TPU v7x, 128 devices: a whole 4x4x4 slice. The times are simulated.
128 devices in a mesh: seg: 8 (over y_lo, z), grp: 16 (over x, y_hi, core).
Axes of the slice: x: 4, y: 4 (y_hi: 2, y_lo: 2; y = y_hi * 2 + y_lo), z: 4, core: 2. Of those that a mesh axis runs over, the one named last changes fastest.
Arguments:
- frames_in: bfloat16 [128, 32, 120, 128], P(('seg', 'grp')), may hold values from -6 to 6
- spatial_weight: bfloat16 [9, 128, 128], replicated, may hold values from -0.1875 to 0.1875
- temporal_weight: bfloat16 [2, 5, 128, 128], replicated, may hold values from -0.25 to 0.25
- uniting_weight: bfloat16 [2, 128, 128], replicated, may hold values from -0.375 to 0.375
- key_index: int32 [8], replicated, may hold values from 0 to 15
- dilation: int32 [2], replicated, may hold values from 1 to 8, as said below
- cotangent: bfloat16 [128, 32, 120, 128], P(('seg', 'grp')), may hold values from -6 to 6
Outputs:
- united: bfloat16 [128, 32, 120, 128], P(('seg', 'grp'))
- grad_frames: bfloat16 [128, 32, 120, 128], P(('seg', 'grp'))
- grad_spatial: float32 [9, 128, 128], replicated
- grad_temporal: float32 [2, 5, 128, 128], replicated
- grad_uniting: float32 [2, 128, 128], replicated
Inputs may be any that keep to these rules, and one draw needn't show every extreme that they name: `key_index`: position of a segment's keyframe within its 16 frames. Exactly one layer uses dilation 8; the others use less.
All inputs are finite; a program needn't handle non-finite values.
Results may differ from a plain program's by a relative error of at most 0.0095.
Values may be sent and summed in bfloat16 or wider, within the bound.
A program may use at most 128 MiB of HBM per device.

v0:
```python
import jax
import jax.numpy as jnp
from jax import lax
from jax.sharding import PartitionSpec as P

LAYERS = 2
DMAX = 8


def from_root(value, axis, root):
    mine = lax.axis_index(axis) == root
    return lax.psum(jnp.where(mine, value, jnp.zeros_like(value)), axis)


def silu_grad(value):
    sigma = jax.nn.sigmoid(value)
    return sigma * (1.0 + value * (1.0 - sigma))


def inner(left, right):
    return lax.dot_general(
        left, right, (((0,), (0,)), ((), ())), preferred_element_type=jnp.float32
    )


def spatial_forward(frames, kernel):
    count, rows, cols, chans = frames.shape
    padded = jnp.pad(frames, ((0, 0), (1, 1), (1, 1), (0, 0)))
    total = jnp.zeros((count * rows * cols, chans), jnp.float32)
    for row_tap in range(3):
        for col_tap in range(3):
            piece = padded[:, row_tap : row_tap + rows, col_tap : col_tap + cols, :].reshape(
                -1, chans
            )
            total = total + jnp.dot(
                piece, kernel[3 * row_tap + col_tap], preferred_element_type=jnp.float32
            )
    return total.reshape(frames.shape)


def spatial_back(grads, kernel):
    count, rows, cols, chans = grads.shape
    padded = jnp.pad(grads, ((0, 0), (1, 1), (1, 1), (0, 0)))
    total = jnp.zeros((count * rows * cols, chans), jnp.float32)
    for row_tap in range(3):
        for col_tap in range(3):
            piece = padded[
                :, 2 - row_tap : 2 - row_tap + rows, 2 - col_tap : 2 - col_tap + cols, :
            ].reshape(-1, chans)
            total = total + jnp.dot(
                piece, kernel[3 * row_tap + col_tap].T, preferred_element_type=jnp.float32
            )
    return total.reshape(grads.shape)


def spatial_wgrad(frames, grads):
    count, rows, cols, chans = frames.shape
    padded = jnp.pad(frames, ((0, 0), (1, 1), (1, 1), (0, 0)))
    flat_grads = grads.reshape(-1, chans)
    result = []
    for row_tap in range(3):
        for col_tap in range(3):
            piece = padded[:, row_tap : row_tap + rows, col_tap : col_tap + cols, :].reshape(
                -1, chans
            )
            result.append(inner(piece, flat_grads))
    return jnp.stack(result)


def shifted(values, offset):
    padded = jnp.pad(values, ((2 * DMAX, 2 * DMAX), (0, 0), (0, 0)))
    start = 2 * DMAX + offset
    return lax.dynamic_slice_in_dim(padded, start, values.shape[0], 0)


def temporal_forward(acts, kernel, step_size):
    chans = acts.shape[2]
    total = jnp.zeros((acts.shape[0] * acts.shape[1], chans), jnp.float32)
    for tap in range(5):
        piece = shifted(acts, (tap - 2) * step_size).reshape(-1, chans)
        total = total + jnp.dot(piece, kernel[tap], preferred_element_type=jnp.float32)
    return total.reshape(acts.shape)


def temporal_back(grads, kernel, step_size):
    chans = grads.shape[2]
    total = jnp.zeros((grads.shape[0] * grads.shape[1], chans), jnp.float32)
    for tap in range(5):
        piece = shifted(grads, (2 - tap) * step_size).reshape(-1, chans)
        total = total + jnp.dot(piece, kernel[tap].T, preferred_element_type=jnp.float32)
    return total.reshape(grads.shape)


def temporal_wgrad(acts, grads, step_size):
    chans = acts.shape[2]
    flat_grads = grads.reshape(-1, chans)
    return jnp.stack(
        [
            inner(shifted(acts, (tap - 2) * step_size).reshape(-1, chans), flat_grads)
            for tap in range(5)
        ]
    )


def to_pixels(flat):
    return lax.all_to_all(flat, ("seg", "grp"), split_axis=1, concat_axis=0, tiled=True)


def to_frames(blocks):
    return lax.all_to_all(blocks, ("seg", "grp"), split_axis=0, concat_axis=1, tiled=True)


def local(
    frames_in, spatial_weight, temporal_weight, uniting_weight, key_index, dilation, cotangent
):
    local_frames, rows, cols, chans = frames_in.shape
    pixels = rows * cols
    seg_count = lax.axis_size("seg")
    pre_spatial = spatial_forward(frames_in, spatial_weight)
    act_zero = jax.nn.silu(pre_spatial).astype(jnp.bfloat16).reshape(local_frames, pixels, chans)
    cot_local = cotangent.reshape(local_frames, pixels, chans)
    act_blocks = to_pixels(act_zero)
    cot_blocks = lax.all_to_all(cot_local, ("seg", "grp"), split_axis=1, concat_axis=0, tiled=True)
    acts = [act_blocks]
    total_frames = acts[0].shape[0]
    block = acts[0].shape[1]
    seg_frames = total_frames // seg_count
    pres = []
    for layer in range(LAYERS):
        pre = temporal_forward(acts[-1], temporal_weight[layer], dilation[layer])
        pres.append(pre)
        acts.append(jax.nn.silu(pre).astype(jnp.bfloat16))
    feat = acts[-1]
    feat_seg = feat.reshape(seg_count, seg_frames, block, chans)
    positions = jnp.arange(seg_frames, dtype=jnp.int32)
    onehot = positions[None, :] == key_index[:, None]
    keys = jnp.einsum(
        "ns,nspc->npc", onehot.astype(jnp.bfloat16), feat_seg, preferred_element_type=jnp.float32
    ).astype(jnp.bfloat16)
    key_full = jnp.broadcast_to(keys[:, None], feat_seg.shape).reshape(-1, chans)
    feat_flat = feat.reshape(-1, chans)
    feat_time = to_frames(feat)
    seg_here = key_index[lax.axis_index("seg")]
    owner = seg_here // local_frames
    local_pos = seg_here % local_frames
    panel = lax.dynamic_index_in_dim(feat_time, local_pos, 0, keepdims=False)
    key_panel = from_root(panel, "grp", owner)
    key_part = jnp.dot(key_panel, uniting_weight[1], preferred_element_type=jnp.float32)
    main_part = jnp.dot(
        feat_time.reshape(-1, chans), uniting_weight[0], preferred_element_type=jnp.float32
    )
    united = (main_part.reshape(local_frames, pixels, chans) + key_part[None]).astype(jnp.bfloat16)
    cot_flat = cot_blocks.reshape(-1, chans)
    grad_feat = jnp.dot(cot_flat, uniting_weight[0].T, preferred_element_type=jnp.float32)
    seg_cot = jnp.sum(
        cot_blocks.reshape(seg_count, seg_frames, block, chans).astype(jnp.float32), axis=1
    )
    key_term = jnp.dot(
        seg_cot.reshape(-1, chans),
        uniting_weight[1].T.astype(jnp.float32),
        precision=lax.Precision.HIGHEST,
    ).reshape(seg_count, 1, block, chans)
    placed = onehot.astype(jnp.float32)[:, :, None, None] * key_term
    grad_feat = grad_feat.reshape(seg_count, seg_frames, block, chans) + placed
    grad_feat = grad_feat.reshape(total_frames, block, chans)
    grad_uniting = jnp.stack([inner(feat_flat, cot_flat), inner(key_full, cot_flat)])
    grad_pre = (grad_feat * silu_grad(pres[-1])).astype(jnp.bfloat16)
    tgrads = [None] * LAYERS
    grad_act0 = None
    for layer in range(LAYERS - 1, -1, -1):
        tgrads[layer] = temporal_wgrad(acts[layer], grad_pre, dilation[layer])
        grad_act = temporal_back(grad_pre, temporal_weight[layer], dilation[layer])
        if layer > 0:
            grad_pre = (grad_act * silu_grad(pres[layer - 1])).astype(jnp.bfloat16)
        else:
            grad_act0 = grad_act.astype(jnp.bfloat16)
    grad_time = to_frames(grad_act0).reshape(frames_in.shape)
    grad_spre = (grad_time.astype(jnp.float32) * silu_grad(pre_spatial)).astype(jnp.bfloat16)
    grad_frames = spatial_back(grad_spre, spatial_weight).astype(jnp.bfloat16)
    grad_spatial = spatial_wgrad(frames_in, grad_spre)
    summed = lax.psum((grad_spatial, jnp.stack(tgrads), grad_uniting), ("seg", "grp"))
    scale = 1.0 / jnp.sqrt(jnp.float32(total_frames * pixels))
    return (
        united.reshape(frames_in.shape),
        grad_frames,
        summed[0] * scale,
        summed[1] * scale,
        summed[2] * scale,
    )


def solution(mesh):
    placed = (
        P(("seg", "grp"), None, None, None),
        P(),
        P(),
        P(),
        P(),
        P(),
        P(("seg", "grp"), None, None, None),
    )
    return jax.shard_map(
        local,
        mesh=mesh,
        in_specs=placed,
        out_specs=(
            P(("seg", "grp"), None, None, None),
            P(("seg", "grp"), None, None, None),
            P(),
            P(),
            P(),
        ),
        check_vma=False,
    )
```

profile of v0, /device:TPU:1, one launch (start us, length us, event | category | flops | bytes accessed | tf_op | source)
XLA Modules:
  0.0 694.7 jit_solution(8917479555947847527)
XLA Ops:
  7.2 7.2 %pad_slice_fusion.8 = (bf16[1,32,120,128]{3,2,1,0:T(8,128)(2,1)S(1)}, bf16[1,32,120,128]{3,2,1,0:T(8,128)(2,1)S(1)}, bf16[1,32,120,128]{3,2,1,0:T(8,128)(2,1)S(1...) fusion(bf16[1,32,120,128]{3,2,1,0:T(8,128)(2,1)} %param.7), kind=kLoop, calls=%fused_computation.144 | loop fusion | bytes 8847360 | tf_op jit(solution)/shard_map/slice | solution.py:32
  19.3 16.0 %copy.215 = bf16[1,3840,128]{2,0,1:T(2,128)(2,1)} copy(bf16[1,3840,128]{2,1,0:T(8,128)(2,1)S(1)} %fusion.41) | data formatting | bytes 1966080 | tf_op jit(solution)/shard_map/convert_element_type | solution.py:120
  35.9 22.2 %reduce.4 = bf16[3840,128]{1,0:T(8,128)(2,1)S(1)} reduce(bf16[3840,1,128]{2,1,0:T(2,128)(2,1)} %bitcast.386, bf16[]{:T(256)} %broadcast.145), dimensions={1}, to_apply=%bitcast.378.reduce_sub_computation | reduce | bytes 1966082
  59.4 11.5 %all-to-all-start = ((bf16[128,2,1920]{2,1,0:T(2,128)(2,1)}), bf16[128,2,1920]{2,1,0:T(2,128)(2,1)S(1)}, u32[]{:S(2)}, u32[]{:S(2)}) async-start(bf16[128,2,1920]{2,1,0:T(2,128)(2,1)} %reshape.558), calls=%async_computation | async-start | bytes 1966080 | tf_op jit(solution)/shard_map/all_to_all | solution.py:106
  79.5 9.9 %copy.214 = bf16[1,3840,128]{2,0,1:T(2,128)(2,1)} copy(bf16[1,3840,128]{2,1,0:T(8,128)(2,1)} %bitcast.404) | data formatting | bytes 1966080 | tf_op jit(solution)/shard_map/reshape | solution.py:121
  89.3 23.1 %reduce.5 = bf16[3840,128]{1,0:T(8,128)(2,1)} reduce(bf16[3840,1,128]{2,1,0:T(2,128)(2,1)} %bitcast.387, bf16[]{:T(256)} %broadcast.145), dimensions={1}, to_apply=%bitcast.377.reduce_sub_computation | reduce | bytes 1966082
  118.8 10.6 %all-to-all-start.2 = ((bf16[128,2,1920]{2,1,0:T(2,128)(2,1)}), bf16[128,2,1920]{2,1,0:T(2,128)(2,1)}, u32[]{:S(2)}, u32[]{:S(2)}) async-start(bf16[128,2,1920]{2,1,0:T(2,128)(2,1)} %reshape.560), calls=%async_computation.2 | async-start | bytes 1966080 | tf_op jit(solution)/shard_map/all_to_all | solution.py:123
  130.2 17.4 %bitcast_reduce_fusion.1 = bf16[3840,128]{1,0:T(8,128)(2,1)} fusion(bf16[3840,1,128]{2,1,0:T(2,128)(2,1)S(1)} %reshape.559), kind=kLoop, calls=%fused_computation.264 | loop fusion | bytes 1966080 | tf_op jit(solution)/shard_map/all_to_all | solution.py:106
  150.6 5.6 pad_dynamic-slice_fusion.12
  188.8 3.5 pad_dynamic-slice_fusion.8
  219.0 4.1 reshape.561
  223.2 17.5 %bitcast_reduce_fusion = bf16[3840,128]{1,0:T(8,128)(2,1)} fusion(bf16[3840,1,128]{2,1,0:T(2,128)(2,1)S(1)} %reshape.561), kind=kLoop, calls=%fused_computation.263 | loop fusion | bytes 1966080 | tf_op jit(solution)/shard_map/all_to_all | solution.py:123
  244.5 5.1 multiply_convert_fusion
  258.1 4.2 multiply_convert_fusion.9
  263.4 3.2 pad_dynamic-slice_fusion.4
  292.0 3.2 multiply_convert_fusion.6
  304.7 3.5 pad_dynamic-slice_fusion
  338.1 10.2 %all-to-all-start.3 = ((bf16[128,30,128]{2,1,0:T(8,128)(2,1)}), bf16[128,30,128]{2,1,0:T(8,128)(2,1)}, u32[]{:S(2)}, u32[]{:S(2)}) async-start(bf16[128,30,128]{2,1,0:T(8,128)(2,1)} %convert_element_type.196), calls=%async_computation.3 | async-start | bytes 2097152 | tf_op jit(solution)/shard_map/all_to_all | solution.py:110
  358.1 8.9 %all-to-all-done.3 = bf16[128,30,128]{2,1,0:T(8,128)(2,1)} async-done(((bf16[128,30,128]{2,1,0:T(8,128)(2,1)}), bf16[128,30,128]{2,1,0:T(8,128)(2,1)}, u32[]{:S(2)}, u32[]{:S(2)}) %all-to-all-start.3) | async-done | bytes 983072 | tf_op jit(solution)/shard_map/all_to_all | solution.py:110
  366.9 4.8 all-to-all-start.1
  378.6 3.2 multiply_convert_fusion.3
  399.0 3.7 pad_slice_fusion
  418.5 128.1 %all-reduce.12.cloned.1.call-done = (f32[9,128,128]{2,1,0:T(8,128)}, f32[2,5,128,128]{3,2,1,0:T(8,128)}, f32[2,128,128]{2,1,0:T(8,128)}) async-done(((f32[9,128,128]{2,1,0:T(8,128)}, f32[2,5,128,128]{3,2,1,0:T(8,128)}, f32[2,128,128]{2,1,0:T(8,128)}), (f32[9,128,128]{2,1,0:T(8,128)}, f32[2,5,128,128]{3,2,1,0:T(8,128)}, f32[2,128,128]{2,1,0:T(8,128)})) %all-reduce.12.cloned.1.call-update) | async-done | bytes 1376272 | tf_op jit(solution)/shard_map/psum | solution.py:181
  552.1 133.0 %all-reduce.10.cloned.1.call-done = bf16[3840,128]{1,0:T(8,128)(2,1)} async-done(((bf16[3840,128]{1,0:T(8,128)(2,1)}), bf16[3840,128]{1,0:T(8,128)(2,1)}) %all-reduce.10.cloned.1.call-update) | async-done | bytes 983056 | tf_op jit(solution)/shard_map/psum | solution.py:12
  (266 shorter events, 212.6 us)
Async XLA Ops:
  7.2 7.2 %copy-start.47 = (bf16[9,128,128]{2,1,0:T(8,128)(2,1)S(1)}, bf16[9,128,128]{2,1,0:T(8,128)(2,1)}, u32[]{:S(2)}) copy-start(bf16[9,128,128]{2,1,0:T(8,128)(2,1)} %param.8) | copy-start | bytes 884740
  18.8 59.2 %copy-start = (f32[3840,128]{1,0:T(8,128)}, f32[3840,128]{1,0:T(8,128)S(1)}, u32[]{:S(2)}) copy-start(f32[3840,128]{1,0:T(8,128)S(1)} %convolution_add_fusion.25) | copy-start | bytes 5898244
  58.1 12.8 %copy-start.57 = (s32[2]{0:T(128)S(1)}, s32[2]{0:T(128)}, u32[]{:S(2)}) copy-start(s32[2]{0:T(128)} %param.12) | copy-start | bytes 28
  59.4 59.4 %all-to-all-start = ((bf16[128,2,1920]{2,1,0:T(2,128)(2,1)}), bf16[128,2,1920]{2,1,0:T(2,128)(2,1)S(1)}, u32[]{:S(2)}, u32[]{:S(2)}) async-start(bf16[128,2,1920]{2,1,0:T(2,128)(2,1)} %reshape.558), calls=%async_computation | async-start | bytes 1966080 | tf_op jit(solution)/shard_map/all_to_all | solution.py:106
  89.3 26.2 %copy-start.23 = (f32[128,30,128]{2,1,0:T(8,128)S(1)}, f32[128,30,128]{2,1,0:T(8,128)}, u32[]{:S(2)}) copy-start(f32[128,30,128]{2,1,0:T(8,128)} %reshape.520) | copy-start | bytes 5898244
  118.8 100.2 %all-to-all-start.2 = ((bf16[128,2,1920]{2,1,0:T(2,128)(2,1)}), bf16[128,2,1920]{2,1,0:T(2,128)(2,1)}, u32[]{:S(2)}, u32[]{:S(2)}) async-start(bf16[128,2,1920]{2,1,0:T(2,128)(2,1)} %reshape.560), calls=%async_computation.2 | async-start | bytes 1966080 | tf_op jit(solution)/shard_map/all_to_all | solution.py:123
  130.2 46.6 %copy-start.6 = (bf16[3840,1,128]{2,1,0:T(2,128)(2,1)}, bf16[3840,1,128]{2,1,0:T(2,128)(2,1)S(1)}, u32[]{:S(2)}) copy-start(bf16[3840,1,128]{2,1,0:T(2,128)(2,1)S(1)} %reshape.559) | copy-start | bytes 2949124
  156.2 4.2 copy-start.10
  160.3 4.9 copy-start.12
  188.3 4.0 copy-start.2
  192.3 4.9 copy-start.19
  197.3 4.1 copy-start.17
  223.1 19.7 %copy-start.24 = (bf16[3840,1,128]{2,1,0:T(2,128)(2,1)}, bf16[3840,1,128]{2,1,0:T(2,128)(2,1)S(1)}, u32[]{:S(2)}) copy-start(bf16[3840,1,128]{2,1,0:T(2,128)(2,1)S(1)} %reshape.561) | copy-start | bytes 2949124
  240.7 3.6 copy-start.56
  258.1 4.2 copy-start.22
  304.7 3.5 copy-start.5
  304.7 3.5 copy-start.25
  311.0 4.8 copy-start.20
  338.1 13.6 %copy-start.7 = (bf16[3840,1,128]{2,1,0:T(2,128)(2,1)S(1)}, bf16[3840,1,128]{2,1,0:T(2,128)(2,1)}, u32[]{:S(2)}) copy-start(bf16[3840,1,128]{2,1,0:T(2,128)(2,1)} %copy-done.6) | copy-start | bytes 2949124
  338.1 28.8 %all-to-all-start.3 = ((bf16[128,30,128]{2,1,0:T(8,128)(2,1)}), bf16[128,30,128]{2,1,0:T(8,128)(2,1)}, u32[]{:S(2)}, u32[]{:S(2)}) async-start(bf16[128,30,128]{2,1,0:T(8,128)(2,1)} %convert_element_type.196), calls=%async_computation.3 | async-start | bytes 2097152 | tf_op jit(solution)/shard_map/all_to_all | solution.py:110
  351.7 3.5 copy-start.11
  366.9 37.4 %all-to-all-start.1 = ((bf16[128,30,128]{2,1,0:T(8,128)(2,1)}), bf16[128,30,128]{2,1,0:T(8,128)(2,1)}, u32[]{:S(2)}, u32[]{:S(2)}) async-start(bf16[128,30,128]{2,1,0:T(8,128)(2,1)} %copy.137), calls=%async_computation.1 | async-start | bytes 2097152 | tf_op jit(solution)/shard_map/all_to_all | solution.py:110
  371.8 174.8 %all-reduce.12.cloned.1.call-start = ((), (), s32[]{:S(2)}) async-start(), calls=%async_computation.5 | async-start | bytes 2752512 | tf_op jit(solution)/shard_map/psum | solution.py:181
  396.2 288.8 %all-reduce.10.cloned.1.call-start = ((), (), s32[]{:S(2)}) async-start(), calls=%async_computation.4 | async-start | bytes 1966080 | tf_op jit(solution)/shard_map/psum | solution.py:12
  (42 other events, 74.7 us)
Sparse Core Ops, SparseCore 0:
  396.3 150.2 all-reduce.11
  549.8 135.1 all-reduce.9
where the time goes:
time: 707 us; the launch traced here: 695 us
  waiting for transfers between devices  270 us (38%)
  local copies, waits for them, and re-layouts  221 us (31%)
  matrix products  74.7 us (11%)
  other arithmetic  69.4 us (10%)
  starting transfers between devices  37.2 us (5%)
  between operations  22.4 us (3%)
    psum x1, waiting for transfers between devices, from_root(): return lax.psum(jnp.where(mine, value, jnp.zeros_like(value)), axis)  133 us
    psum x1, waiting for transfers between devices, local(): lax.psum((grad_spatial, jnp.stack(tgrads), grad_uniting), ('seg', 'grp'))  128 us
    dynamic_slice x20, local copies, waits for them, and re-layouts, shifted(): return lax.dynamic_slice_in_dim(padded, start, values.shape[0], 0)  50.3 us
    unnamed x2, other arithmetic  45.3 us
    dot_general x21, matrix products, inner(): lax.dot_general(left, right, (((0,), (0,)), ((), ())), preferred_element_...  24 us
    all_to_all x3, local copies, waits for them, and re-layouts, to_pixels(): lax.all_to_all(flat, ('seg', 'grp'), split_axis=1, concat_axis=0, tiled=T...  20.4 us
    unnamed x125, local copies, waits for them, and re-layouts  18.4 us
    all_to_all x1, local copies, waits for them, and re-layouts, local(): lax.all_to_all(cot_local, ('seg', 'grp'), split_axis=1, concat_axis=0, ti...  17.5 us
  transfers between devices with their start and end apart: 6, of which 3 were waited for; matrix products, arithmetic and copies ran while one was open for 27% of the time, Pallas kernels for 0%

commit v1 on v0

--- a/solution.py
+++ b/solution.py
@@ -110,6 +110,25 @@
     return lax.all_to_all(blocks, ("seg", "grp"), split_axis=0, concat_axis=1, tiled=True)
 
 
+def all_sum(parts):
+    flat = jnp.concatenate([p.reshape(-1) for p in parts])
+    count = lax.axis_size(("seg", "grp"))
+    chunk = flat.shape[0] // count
+    pieces = lax.all_to_all(
+        flat.reshape(count, chunk), ("seg", "grp"), split_axis=0, concat_axis=0, tiled=True
+    )
+    mine = jnp.sum(pieces, axis=0)
+    spread = jnp.broadcast_to(mine[None], (count, chunk))
+    whole = lax.all_to_all(spread, ("seg", "grp"), split_axis=0, concat_axis=0, tiled=True)
+    whole = whole.reshape(-1)
+    out = []
+    offset = 0
+    for p in parts:
+        out.append(whole[offset : offset + p.size].reshape(p.shape))
+        offset += p.size
+    return out
+
+
 def local(
     frames_in, spatial_weight, temporal_weight, uniting_weight, key_index, dilation, cotangent
 ):
@@ -120,7 +139,7 @@
     act_zero = jax.nn.silu(pre_spatial).astype(jnp.bfloat16).reshape(local_frames, pixels, chans)
     cot_local = cotangent.reshape(local_frames, pixels, chans)
     act_blocks = to_pixels(act_zero)
-    cot_blocks = lax.all_to_all(cot_local, ("seg", "grp"), split_axis=1, concat_axis=0, tiled=True)
+    cot_blocks = to_pixels(cot_local)
     acts = [act_blocks]
     total_frames = acts[0].shape[0]
     block = acts[0].shape[1]
@@ -139,17 +158,14 @@
     ).astype(jnp.bfloat16)
     key_full = jnp.broadcast_to(keys[:, None], feat_seg.shape).reshape(-1, chans)
     feat_flat = feat.reshape(-1, chans)
-    feat_time = to_frames(feat)
-    seg_here = key_index[lax.axis_index("seg")]
-    owner = seg_here // local_frames
-    local_pos = seg_here % local_frames
-    panel = lax.dynamic_index_in_dim(feat_time, local_pos, 0, keepdims=False)
-    key_panel = from_root(panel, "grp", owner)
-    key_part = jnp.dot(key_panel, uniting_weight[1], preferred_element_type=jnp.float32)
-    main_part = jnp.dot(
-        feat_time.reshape(-1, chans), uniting_weight[0], preferred_element_type=jnp.float32
-    )
-    united = (main_part.reshape(local_frames, pixels, chans) + key_part[None]).astype(jnp.bfloat16)
+    key_part = jnp.dot(
+        keys.reshape(-1, chans), uniting_weight[1], preferred_element_type=jnp.float32
+    ).reshape(seg_count, 1, block, chans)
+    main_part = jnp.dot(feat_flat, uniting_weight[0], preferred_element_type=jnp.float32)
+    united_blocks = (
+        main_part.reshape(seg_count, seg_frames, block, chans) + key_part
+    ).astype(jnp.bfloat16).reshape(total_frames, block, chans)
+    united = to_frames(united_blocks)
     cot_flat = cot_blocks.reshape(-1, chans)
     grad_feat = jnp.dot(cot_flat, uniting_weight[0].T, preferred_element_type=jnp.float32)
     seg_cot = jnp.sum(
@@ -178,7 +194,7 @@
     grad_spre = (grad_time.astype(jnp.float32) * silu_grad(pre_spatial)).astype(jnp.bfloat16)
     grad_frames = spatial_back(grad_spre, spatial_weight).astype(jnp.bfloat16)
     grad_spatial = spatial_wgrad(frames_in, grad_spre)
-    summed = lax.psum((grad_spatial, jnp.stack(tgrads), grad_uniting), ("seg", "grp"))
+    summed = all_sum((grad_spatial, jnp.stack(tgrads), grad_uniting))
     scale = 1.0 / jnp.sqrt(jnp.float32(total_frames * pixels))
     return (
         united.reshape(frames_in.shape),

time: 707 us -> 502 us (0.71)
  waiting for transfers between devices: 270 us -> 36.5 us
  starting transfers between devices: 37.2 us -> 53.4 us
  between operations: 22.4 us -> 8.25 us
  local copies, waits for them, and re-layouts: 221 us -> 235 us
  matrix products: 74.7 us -> 87.9 us
    psum x2 -> x0, waiting for transfers between devices: 261 us -> none  [the longest x1 133 us: from_root(): return lax.psum(jnp.where(mine, value, jnp.zeros_like(value)), axis)]
    all_to_all x1 -> x2, waiting for transfers between devices: 0.01 us -> 23.5 us  [the longest x1 15.9 us: all_sum(): lax.all_to_all(spread, ('seg', 'grp'), split_axis=0, concat_axis=0, tiled...]
    all_to_all x3 -> x4, local copies, waits for them, and re-layouts: 20.4 us -> 40.8 us  [to_pixels(): lax.all_to_all(flat, ('seg', 'grp'), split_axis=1, concat_axis=0, tiled=T...]
    all_to_all x1 -> x0, local copies, waits for them, and re-layouts: 17.5 us -> none  [local(): lax.all_to_all(cot_local, ('seg', 'grp'), split_axis=1, concat_axis=0, ti...]
    all_to_all x1 -> x2, starting transfers between devices: 11.5 us -> 23 us  [to_pixels(): lax.all_to_all(flat, ('seg', 'grp'), split_axis=1, concat_axis=0, tiled=T...]
    dot_general x9, matrix products: 8.35 us -> 17 us  [spatial_back(): jnp.dot(piece, kernel[3 * row_tap + col_tap].T, preferred_element_type=jn...]
    all_to_all x1 -> x2, starting transfers between devices: 10.6 us -> 14.9 us  [the longest x1 10.6 us: all_sum(): lax.all_to_all(flat.reshape(count, chunk), ('seg', 'grp'), split_axis=0,...]
    unnamed x125 -> x113, local copies, waits for them, and re-layouts: 18.4 us -> 21.1 us
  transfers between devices with their start and end apart: 6 -> 6, of which waited for: 3 -> 3; matrix products, arithmetic and copies ran while one was open for 27% -> 40% of each run, Pallas kernels for 0% -> 0%
where the time goes in v1:
time: 502 us; the launch traced here: 492 us
  local copies, waits for them, and re-layouts  235 us (47%)
  matrix products  87.9 us (18%)
  other arithmetic  70.9 us (14%)
  starting transfers between devices  53.4 us (11%)
  waiting for transfers between devices  36.5 us (7%)
  between operations  8.25 us (2%)
    dynamic_slice x20, local copies, waits for them, and re-layouts, shifted(): return lax.dynamic_slice_in_dim(padded, start, values.shape[0], 0)  53.4 us
    unnamed x2, other arithmetic  46.2 us
    all_to_all x4, local copies, waits for them, and re-layouts, to_pixels(): lax.all_to_all(flat, ('seg', 'grp'), split_axis=1, concat_axis=0, tiled=T...  40.8 us
    dot_general x21, matrix products, inner(): lax.dot_general(left, right, (((0,), (0,)), ((), ())), preferred_element_...  28.1 us
    all_to_all x2, starting transfers between devices, to_pixels(): lax.all_to_all(flat, ('seg', 'grp'), split_axis=1, concat_axis=0, tiled=T...  23 us
    unnamed x113, local copies, waits for them, and re-layouts  21.1 us
    dot_general x9, matrix products, spatial_back(): jnp.dot(piece, kernel[3 * row_tap + col_tap].T, preferred_element_type=jn...  17 us
    dot_general x10, matrix products, temporal_back(): jnp.dot(piece, kernel[tap].T, preferred_element_type=jnp.float32)  16.8 us
  transfers between devices with their start and end apart: 6, of which 3 were waited for; matrix products, arithmetic and copies ran while one was open for 40% of the time, Pallas kernels for 0%

profile of v1, /device:TPU:1, one launch (start us, length us, event | category | flops | bytes accessed | tf_op | source)
XLA Modules:
  0.0 491.9 jit_solution(17420087802253160140)
XLA Ops:
  0.6 7.3 %pad_slice_fusion.8 = (bf16[1,32,120,128]{3,2,1,0:T(8,128)(2,1)S(1)}, bf16[1,32,120,128]{3,2,1,0:T(8,128)(2,1)S(1)}, bf16[1,32,120,128]{3,2,1,0:T(8,128)(2,1)S(1...) fusion(bf16[1,32,120,128]{3,2,1,0:T(8,128)(2,1)} %param.7), kind=kLoop, calls=%fused_computation.142 | loop fusion | bytes 8847360 | tf_op jit(solution)/shard_map/slice | solution.py:32
  12.9 16.0 %copy.296 = bf16[1,3840,128]{2,0,1:T(2,128)(2,1)} copy(bf16[1,3840,128]{2,1,0:T(8,128)(2,1)S(1)} %fusion.40) | data formatting | bytes 1966080 | tf_op jit(solution)/shard_map/convert_element_type | solution.py:139
  29.5 23.1 %reduce.5 = bf16[3840,128]{1,0:T(8,128)(2,1)} reduce(bf16[3840,1,128]{2,1,0:T(2,128)(2,1)} %bitcast.395, bf16[]{:T(256)} %broadcast.150), dimensions={1}, to_apply=%bitcast.387.reduce_sub_computation | reduce | bytes 1966082
  55.6 12.3 %all-to-all-start = ((bf16[128,2,1920]{2,1,0:T(2,128)(2,1)}), bf16[128,2,1920]{2,1,0:T(2,128)(2,1)}, u32[]{:S(2)}, u32[]{:S(2)}) async-start(bf16[128,2,1920]{2,1,0:T(2,128)(2,1)} %reshape.597), calls=%async_computation | async-start | bytes 1966080 | tf_op jit(solution)/shard_map/all_to_all | solution.py:106
  76.5 9.9 %copy.295 = bf16[1,3840,128]{2,0,1:T(2,128)(2,1)} copy(bf16[1,3840,128]{2,1,0:T(8,128)(2,1)} %bitcast.418) | data formatting | bytes 1966080 | tf_op jit(solution)/shard_map/reshape | solution.py:140
  86.4 23.1 %reduce.6 = bf16[3840,128]{1,0:T(8,128)(2,1)} reduce(bf16[3840,1,128]{2,1,0:T(2,128)(2,1)} %bitcast.396, bf16[]{:T(256)} %broadcast.150), dimensions={1}, to_apply=%bitcast.386.reduce_sub_computation | reduce | bytes 1966082
  114.4 10.7 %all-to-all-start.2 = ((bf16[128,2,1920]{2,1,0:T(2,128)(2,1)}), bf16[128,2,1920]{2,1,0:T(2,128)(2,1)}, u32[]{:S(2)}, u32[]{:S(2)}) async-start(bf16[128,2,1920]{2,1,0:T(2,128)(2,1)} %reshape.599), calls=%async_computation.2 | async-start | bytes 1966080 | tf_op jit(solution)/shard_map/all_to_all | solution.py:106
  125.2 4.1 reshape.598
  129.4 17.4 %bitcast_reduce_fusion.1 = bf16[3840,128]{1,0:T(8,128)(2,1)} fusion(bf16[3840,1,128]{2,1,0:T(2,128)(2,1)S(1)} %reshape.598), kind=kLoop, calls=%fused_computation.260 | loop fusion | bytes 1966080 | tf_op jit(solution)/shard_map/all_to_all | solution.py:106
  151.5 5.9 %pad_dynamic-slice_fusion.12 = (bf16[128,30,128]{0,2,1:T(8,128)(2,1)}, bf16[128,30,128]{0,2,1:T(8,128)(2,1)}, bf16[128,30,128]{0,2,1:T(8,128)(2,1)}, bf16[128,30,128]{0,2,1:T(8,128)(2,1)}) fusion(s32[]{:T(128)S(6)} %select_n.19, bf16[128,30,128]{0,2,1:T(8,128)(2,1)} %copy.205, s32[]{:T(128)S(6)} %select_n.17, s32[]{:T(128)S(6)} %select_n.18, s32[]{:T(128)S(6)} %select_n.16), kind=kLoop, calls=%fused_computation.46 | loop fusion | bytes 4915216 | tf_op jit(solution)/shard_map/dynamic_slice | solution.py:73
  222.8 5.7 %reshape.600 = bf16[3840,1,128]{2,1,0:T(2,128)(2,1)} reshape(bf16[128,2,1920]{2,1,0:T(2,128)(2,1)} %all-to-all-done.2) | data formatting | bytes 1966080
  228.5 18.6 %bitcast_reduce_fusion = bf16[3840,128]{1,0:T(8,128)(2,1)} fusion(bf16[3840,1,128]{2,1,0:T(2,128)(2,1)} %reshape.600), kind=kLoop, calls=%fused_computation.259 | loop fusion | bytes 1966080 | tf_op jit(solution)/shard_map/all_to_all | solution.py:106
  250.9 5.0 %multiply_convert_fusion = (bf16[8,16,30,128]{3,2,1,0:T(8,128)(2,1)}, bf16[8,16,30,128]{3,2,1,0:T(8,128)(2,1)}, f32[8,16,30,128]{3,2,1,0:T(8,128)}) fusion(f32[8,16,30,128]{3,2,1,0:T(8,128)} %reshape.530, f32[8,30,128]{2,1,0:T(8,128)S(1)} %fusion.47, f32[8,16]{1,0:T(8,128)S(1)} %get-tuple-element.39, bf16[8,16,30,128]{3,2,1,0:T(8,128)(2,1)} %dot_general.221, ...), kind=kOutput, calls=%fused_computation.50 | convolution fusion | flops 132218880 | bytes 7049216 | tf_op jit(solution)/shard_map/dot_general | solution.py:170
  309.1 3.5 pad_dynamic-slice_fusion
  355.3 10.2 %all-to-all-start.3 = ((bf16[128,30,128]{2,1,0:T(8,128)(2,1)}), bf16[128,30,128]{2,1,0:T(8,128)(2,1)}, u32[]{:S(2)}, u32[]{:S(2)}) async-start(bf16[128,30,128]{2,1,0:T(8,128)(2,1)} %convert_element_type.195), calls=%async_computation.3 | async-start | bytes 2097152 | tf_op jit(solution)/shard_map/all_to_all | solution.py:110
  371.1 13.0 %all-to-all-done.3 = bf16[128,30,128]{2,1,0:T(8,128)(2,1)} async-done(((bf16[128,30,128]{2,1,0:T(8,128)(2,1)}), bf16[128,30,128]{2,1,0:T(8,128)(2,1)}, u32[]{:S(2)}, u32[]{:S(2)}) %all-to-all-start.3) | async-done | bytes 983072 | tf_op jit(solution)/shard_map/all_to_all | solution.py:110
  384.1 5.2 %all-to-all-start.1 = ((bf16[128,30,128]{2,1,0:T(8,128)(2,1)}), bf16[128,30,128]{2,1,0:T(8,128)(2,1)}, u32[]{:S(2)}, u32[]{:S(2)}) async-start(bf16[128,30,128]{2,1,0:T(8,128)(2,1)} %bitcast.52), calls=%async_computation.1 | async-start | bytes 2097152 | tf_op jit(solution)/shard_map/all_to_all | solution.py:110
  394.0 4.2 multiply_convert_fusion.2
  420.4 3.6 pad_slice_fusion
  425.7 10.6 %all-to-all-start.4 = ((f32[128,1,2688]{2,1,0:T(1,128)}), f32[128,1,2688]{2,1,0:T(1,128)}, u32[]{:S(2)}, u32[]{:S(2)}) async-start(f32[128,1,2688]{2,1,0:T(1,128)} %bitcast.397), calls=%async_computation.4 | async-start | bytes 2752512 | tf_op jit(solution)/shard_map/all_to_all | solution.py:117
  436.4 3.6 convolution_add_fusion.7
  450.8 7.6 %all-to-all-done.4 = f32[128,1,2688]{2,1,0:T(1,128)} async-done(((f32[128,1,2688]{2,1,0:T(1,128)}), f32[128,1,2688]{2,1,0:T(1,128)}, u32[]{:S(2)}, u32[]{:S(2)}) %all-to-all-start.4) | async-done | bytes 1376288 | tf_op jit(solution)/shard_map/all_to_all | solution.py:117
  462.4 4.3 all-to-all-start.5
  473.4 15.9 %all-to-all-done.5 = f32[128,1,2688]{2,1,0:T(1,128)S(1)} async-done(((f32[128,1,2688]{2,1,0:T(1,128)}), f32[128,1,2688]{2,1,0:T(1,128)S(1)}, u32[]{:S(2)}, u32[]{:S(2)}) %all-to-all-start.5) | async-done | bytes 1376288 | tf_op jit(solution)/shard_map/all_to_all | solution.py:122
  (253 shorter events, 242.8 us)
Async XLA Ops:
  0.6 7.3 %copy-start.40 = (bf16[9,128,128]{2,1,0:T(8,128)(2,1)S(1)}, bf16[9,128,128]{2,1,0:T(8,128)(2,1)}, u32[]{:S(2)}) copy-start(bf16[9,128,128]{2,1,0:T(8,128)(2,1)} %param.8) | copy-start | bytes 884740
  12.4 62.6 %copy-start = (f32[3840,128]{1,0:T(8,128)}, f32[3840,128]{1,0:T(8,128)S(1)}, u32[]{:S(2)}) copy-start(f32[3840,128]{1,0:T(8,128)S(1)} %convolution_add_fusion.24) | copy-start | bytes 5898244
  52.6 15.3 %copy-start.51 = (s32[2]{0:T(128)S(1)}, s32[2]{0:T(128)}, u32[]{:S(2)}) copy-start(s32[2]{0:T(128)} %param.12) | copy-start | bytes 28
  55.6 58.8 %all-to-all-start = ((bf16[128,2,1920]{2,1,0:T(2,128)(2,1)}), bf16[128,2,1920]{2,1,0:T(2,128)(2,1)}, u32[]{:S(2)}, u32[]{:S(2)}) async-start(bf16[128,2,1920]{2,1,0:T(2,128)(2,1)} %reshape.597), calls=%async_computation | async-start | bytes 1966080 | tf_op jit(solution)/shard_map/all_to_all | solution.py:106
  86.4 26.1 %copy-start.18 = (f32[128,30,128]{2,1,0:T(8,128)S(1)}, f32[128,30,128]{2,1,0:T(8,128)}, u32[]{:S(2)}) copy-start(f32[128,30,128]{2,1,0:T(8,128)} %reshape.556) | copy-start | bytes 5898244
  114.4 108.4 %all-to-all-start.2 = ((bf16[128,2,1920]{2,1,0:T(2,128)(2,1)}), bf16[128,2,1920]{2,1,0:T(2,128)(2,1)}, u32[]{:S(2)}, u32[]{:S(2)}) async-start(bf16[128,2,1920]{2,1,0:T(2,128)(2,1)} %reshape.599), calls=%async_computation.2 | async-start | bytes 1966080 | tf_op jit(solution)/shard_map/all_to_all | solution.py:106
  129.4 50.3 %copy-start.4 = (bf16[3840,1,128]{2,1,0:T(2,128)(2,1)}, bf16[3840,1,128]{2,1,0:T(2,128)(2,1)S(1)}, u32[]{:S(2)}) copy-start(bf16[3840,1,128]{2,1,0:T(2,128)(2,1)S(1)} %reshape.598) | copy-start | bytes 2949124
  191.2 4.1 copy-start.3
  195.3 4.9 copy-start.14
  200.2 4.2 copy-start.12
  204.3 3.4 copy-start.16
  247.1 3.6 copy-start.49
  321.6 3.1 copy-start.15
  321.6 4.1 copy-start.41
  321.6 4.1 copy-start.53
  353.0 13.5 %copy-start.7 = (bf16[128,30,128]{0,2,1:T(8,128)(2,1)S(1)}, bf16[128,30,128]{0,2,1:T(8,128)(2,1)}, u32[]{:S(2)}) copy-start(bf16[128,30,128]{0,2,1:T(8,128)(2,1)} %get-tuple-element.27) | copy-start | bytes 2949124
  355.3 28.8 %all-to-all-start.3 = ((bf16[128,30,128]{2,1,0:T(8,128)(2,1)}), bf16[128,30,128]{2,1,0:T(8,128)(2,1)}, u32[]{:S(2)}, u32[]{:S(2)}) async-start(bf16[128,30,128]{2,1,0:T(8,128)(2,1)} %convert_element_type.195), calls=%async_computation.3 | async-start | bytes 2097152 | tf_op jit(solution)/shard_map/all_to_all | solution.py:110
  365.5 3.9 copy-start.50
  365.5 4.1 copy-start.21
  384.1 41.6 %all-to-all-start.1 = ((bf16[128,30,128]{2,1,0:T(8,128)(2,1)}), bf16[128,30,128]{2,1,0:T(8,128)(2,1)}, u32[]{:S(2)}, u32[]{:S(2)}) async-start(bf16[128,30,128]{2,1,0:T(8,128)(2,1)} %bitcast.52), calls=%async_computation.1 | async-start | bytes 2097152 | tf_op jit(solution)/shard_map/all_to_all | solution.py:110
  394.0 20.2 %copy-start.2 = (f32[128,30,128]{2,1,0:T(8,128)}, f32[128,30,128]{2,1,0:T(8,128)S(1)}, u32[]{:S(2)}) copy-start(f32[128,30,128]{2,1,0:T(8,128)S(1)} %copy.231) | copy-start | bytes 5898244
  425.7 32.7 %all-to-all-start.4 = ((f32[128,1,2688]{2,1,0:T(1,128)}), f32[128,1,2688]{2,1,0:T(1,128)}, u32[]{:S(2)}, u32[]{:S(2)}) async-start(f32[128,1,2688]{2,1,0:T(1,128)} %bitcast.397), calls=%async_computation.4 | async-start | bytes 2752512 | tf_op jit(solution)/shard_map/all_to_all | solution.py:117
  460.6 6.1 %copy-start.23 = (bf16[1,32,120,128]{3,2,1,0:T(8,128)(2,1)S(1)}, bf16[1,32,120,128]{3,2,1,0:T(8,128)(2,1)}, u32[]{:S(2)}) copy-start(bf16[1,32,120,128]{3,2,1,0:T(8,128)(2,1)} %get-tuple-element.11) | copy-start | bytes 2949124
  462.4 26.8 %all-to-all-start.5 = ((f32[128,1,2688]{2,1,0:T(1,128)}), f32[128,1,2688]{2,1,0:T(1,128)S(1)}, u32[]{:S(2)}, u32[]{:S(2)}) async-start(f32[128,1,2688]{2,1,0:T(1,128)} %broadcast_in_dim.5), calls=%async_computation.5 | async-start | bytes 2752512 | tf_op jit(solution)/shard_map/all_to_all | solution.py:122
  (36 other events, 65.9 us)
